TPU v7x, 512 devices: a whole 4x8x8 slice. The times are simulated.
512 devices in a mesh: wide: 64 (over y, z_lo, core), rep: 8 (over z_hi, x).
Axes of the slice: x: 4, y: 8, z: 8 (z_hi: 2, z_lo: 4; z = z_hi * 4 + z_lo), core: 2. Of those that a mesh axis runs over, the one named last changes fastest.
Arguments:
- features: bfloat16 [65536, 512], P(('wide', 'rep')), may hold values from -6 to 6
- w_query: bfloat16 [512, 512], replicated, may hold values from -0.25 to 0.25
- w_key: bfloat16 [512, 512], replicated, may hold values from -0.25 to 0.25
- w_out: bfloat16 [512, 512], replicated, may hold values from -0.25 to 0.25
- edge_weight: bfloat16 [64, 8, 96, 128, 128], P('wide', 'rep'), may hold values from -0.23925781 to 0.23925781
- tile_slot: int32 [64, 8, 96], P('wide', 'rep'), may hold values from 0 to 511, as said below
- tile_count: int32 [64, 8], P('wide', 'rep'), may hold values from 1 to 96, as said below
Outputs:
- updated: bfloat16 [65536, 512], P(('wide', 'rep'))
Inputs may be any that keep to these rules, and one draw needn't show every extreme that they name: For each w and r the first tile_count[w, r] entries of tile_slot[w, r] are distinct and ascending; all 96 entries of a list are distinct. `tile_count`: some device has 96 live tiles.
All inputs are finite; a program needn't handle non-finite values.
Results may differ from a plain program's by a relative error of at most 0.014.
Values may be sent and summed in bfloat16 or wider, within the bound.
A program may use at most 64 MiB of HBM per device.

v0:
```python
import jax
import jax.numpy as jnp
from jax import lax
from jax.sharding import PartitionSpec as P


def from_behind(block, axis, distance):
    devices = range(lax.axis_size(axis))
    route = [((i - distance) % len(devices), i) for i in devices]
    return lax.ppermute(block, axis, route)


def on_device(features, w_query, w_key, w_out, edge_weight, tile_slot, tile_count):
    tile_rows = features.shape[0]
    feat_width = features.shape[1]
    n_wide = lax.axis_size("wide")
    n_rep = lax.axis_size("rep")
    query_rows = jnp.dot(features, w_query, preferred_element_type=jnp.float32).astype(jnp.bfloat16)
    key_rows = jnp.dot(features, w_key, preferred_element_type=jnp.float32).astype(jnp.bfloat16)
    receivers = lax.all_gather(query_rows, "rep", axis=0, tiled=True)
    tile_slots = tile_slot[0, 0]
    live_count = tile_count[0, 0]
    weights = edge_weight[0, 0]
    step_of = tile_slots // n_rep
    active = jnp.arange(tile_slots.shape[0], dtype=jnp.int32) < live_count
    below = step_of[None, :] < jnp.arange(n_wide + 1, dtype=jnp.int32)[:, None]
    bounds = jnp.sum((active[None, :] & below).astype(jnp.int32), axis=1)
    factor = 1.0 / float(feat_width) ** 0.5

    def one_tile(tile_num, sender, partial_value):
        block = tile_slots[tile_num] % n_rep
        targets = lax.dynamic_slice_in_dim(receivers, block * tile_rows, tile_rows, 0)
        scores = (
            lax.dot_general(
                targets, sender, (((1,), (1,)), ((), ())), preferred_element_type=jnp.float32
            )
            * factor
        )
        weighted = (jnp.tanh(scores) * weights[tile_num].astype(jnp.float32)).astype(jnp.bfloat16)
        contrib = jnp.dot(weighted, sender, preferred_element_type=jnp.float32)
        previous = lax.dynamic_slice_in_dim(partial_value, block * tile_rows, tile_rows, 0)
        return lax.dynamic_update_slice_in_dim(
            partial_value, previous + contrib, block * tile_rows, 0
        )

    def one_step(step_num, sender, partial_value):
        return lax.fori_loop(
            bounds[step_num],
            bounds[step_num + 1],
            lambda tile_num, acc: one_tile(tile_num, sender, acc),
            partial_value,
        )

    partial_value = jnp.zeros((n_rep * tile_rows, feat_width), jnp.float32)
    partial_value = one_step(0, key_rows, partial_value)

    def advance(step_num, state_pair):
        sender = from_behind(state_pair[0], "wide", 1)
        return (sender, one_step(step_num, sender, state_pair[1]))

    partial_value = lax.fori_loop(1, n_wide, advance, (key_rows, partial_value))[1]
    summed = lax.psum_scatter(
        partial_value.astype(jnp.bfloat16), "rep", scatter_dimension=0, tiled=True
    )
    mixed = features.astype(jnp.float32) + jnp.dot(
        summed, w_out, preferred_element_type=jnp.float32
    )
    return mixed.astype(jnp.bfloat16)


def solution(mesh):
    in_specs = (
        P(("wide", "rep"), None),
        P(),
        P(),
        P(),
        P("wide", "rep", None, None, None),
        P("wide", "rep", None),
        P("wide", "rep"),
    )
    out_specs = P(("wide", "rep"), None)
    return jax.shard_map(
        on_device, mesh=mesh, in_specs=in_specs, out_specs=out_specs, check_vma=False
    )
```

profile of v0, /device:TPU:1, one launch (start us, length us, event | category | flops | bytes accessed | tf_op | source)
XLA Modules:
  0.0 1935.5 jit_solution(4528999640472336238)
XLA Ops:
  12.8 68.9 %all-gather.2.cloned.1.call-done = bf16[1024,512]{1,0:T(8,128)(2,1)} async-done(((bf16[128,512]{1,0:T(8,128)(2,1)}), bf16[1024,512]{1,0:T(8,128)(2,1)}) %all-gather.2.cloned.1.call-update) | async-done | bytes 1048592 | tf_op jit(solution)/shard_map/all_gather | solution.py:20
  83.2 1705.0 %while.66 = (s32[]{:T(128)}, bf16[128,512]{1,0:T(8,128)(2,1)S(1)}, f32[1024,512]{1,0:T(8,128)S(1)}, s32[65]{0:T(128)S(1)}, s32[96]{0:T(128)S(1)}, /*index=5*/bf1...) while((s32[]{:T(128)}, bf16[128,512]{1,0:T(8,128)(2,1)S(1)}, ...), condition=%wide.region_6.7_spmd, body=%wide.region_3.6_spmd.sunk | while | flops 33685532 | bytes 1739011 | solution.py:61
  83.2 21.4 %collective-permute-start = (bf16[128,512]{1,0:T(8,128)(2,1)S(1)}, bf16[128,512]{1,0:T(8,128)(2,1)S(1)}, u32[]{:S(2)}, u32[]{:S(2)}) collective-permute-start(bf16[128,512]{1,0:T(8,128)(2,1)S(1)} %get-tuple-element.784), channel_id=1, source_target_pairs={{504,0},{0,8},{8,16},{16,24},{24,32},{32,40},{40,48},{48,56},{56,6... | collective-permute-start | bytes 393224 | tf_op jit(solution)/shard_map/while/body/eval_jaxpr/ppermute | solution.py:10
  121.1 20.7 %collective-permute-done = bf16[128,512]{1,0:T(8,128)(2,1)S(1)} collective-permute-done((bf16[128,512]{1,0:T(8,128)(2,1)S(1)}, bf16[128,512]{1,0:T(8,128)(2,1)S(1)}, u32[]{:S(2)}, u32[]{:S(2)}) %collective-permute-start) | collective-permute-done | bytes 131104 | tf_op jit(solution)/shard_map/while/body/eval_jaxpr/ppermute | solution.py:10
  154.0 16.0 collective-permute-done
  193.6 34.7 %collective-permute-done = bf16[128,512]{1,0:T(8,128)(2,1)S(1)} collective-permute-done((bf16[128,512]{1,0:T(8,128)(2,1)S(1)}, bf16[128,512]{1,0:T(8,128)(2,1)S(1)}, u32[]{:S(2)}, u32[]{:S(2)}) %collective-permute-start) | collective-permute-done | bytes 131104 | tf_op jit(solution)/shard_map/while/body/eval_jaxpr/ppermute | solution.py:10
  232.1 24.4 %collective-permute-done = bf16[128,512]{1,0:T(8,128)(2,1)S(1)} collective-permute-done((bf16[128,512]{1,0:T(8,128)(2,1)S(1)}, bf16[128,512]{1,0:T(8,128)(2,1)S(1)}, u32[]{:S(2)}, u32[]{:S(2)}) %collective-permute-start) | collective-permute-done | bytes 131104 | tf_op jit(solution)/shard_map/while/body/eval_jaxpr/ppermute | solution.py:10
  268.6 16.0 collective-permute-done
  284.7 17.9 while.67
  305.1 16.0 collective-permute-done
  353.1 16.0 collective-permute-done
  392.7 24.4 %collective-permute-done = bf16[128,512]{1,0:T(8,128)(2,1)S(1)} collective-permute-done((bf16[128,512]{1,0:T(8,128)(2,1)S(1)}, bf16[128,512]{1,0:T(8,128)(2,1)S(1)}, u32[]{:S(2)}, u32[]{:S(2)}) %collective-permute-start) | collective-permute-done | bytes 131104 | tf_op jit(solution)/shard_map/while/body/eval_jaxpr/ppermute | solution.py:10
  428.5 26.3 %while.67 = (s32[]{:T(128)}, f32[1024,512]{1,0:T(8,128)S(1)}, s32[]{:T(128)}, s32[96]{0:T(128)S(1)}, bf16[1024,512]{1,0:T(8,128)(2,1)}, /*index=5*/bf16[128,512]...) while((s32[]{:T(128)}, f32[1024,512]{1,0:T(8,128)S(1)}, ...), condition=%wide.region_5.5_spmd, body=%wide.region_4.4_spmd.sunk | while | flops 33685524 | bytes 952142 | solution.py:47
  473.3 21.9 %collective-permute-done = bf16[128,512]{1,0:T(8,128)(2,1)S(1)} collective-permute-done((bf16[128,512]{1,0:T(8,128)(2,1)S(1)}, bf16[128,512]{1,0:T(8,128)(2,1)S(1)}, u32[]{:S(2)}, u32[]{:S(2)}) %collective-permute-start) | collective-permute-done | bytes 131104 | tf_op jit(solution)/shard_map/while/body/eval_jaxpr/ppermute | solution.py:10
  514.9 21.9 %collective-permute-done = bf16[128,512]{1,0:T(8,128)(2,1)S(1)} collective-permute-done((bf16[128,512]{1,0:T(8,128)(2,1)S(1)}, bf16[128,512]{1,0:T(8,128)(2,1)S(1)}, u32[]{:S(2)}, u32[]{:S(2)}) %collective-permute-start) | collective-permute-done | bytes 131104 | tf_op jit(solution)/shard_map/while/body/eval_jaxpr/ppermute | solution.py:10
  556.6 17.9 while.67
  588.6 32.7 %collective-permute-done = bf16[128,512]{1,0:T(8,128)(2,1)S(1)} collective-permute-done((bf16[128,512]{1,0:T(8,128)(2,1)S(1)}, bf16[128,512]{1,0:T(8,128)(2,1)S(1)}, u32[]{:S(2)}, u32[]{:S(2)}) %collective-permute-start) | collective-permute-done | bytes 131104 | tf_op jit(solution)/shard_map/while/body/eval_jaxpr/ppermute | solution.py:10
  633.4 16.0 collective-permute-done
  669.1 19.9 %collective-permute-done = bf16[128,512]{1,0:T(8,128)(2,1)S(1)} collective-permute-done((bf16[128,512]{1,0:T(8,128)(2,1)S(1)}, bf16[128,512]{1,0:T(8,128)(2,1)S(1)}, u32[]{:S(2)}, u32[]{:S(2)}) %collective-permute-start) | collective-permute-done | bytes 131104 | tf_op jit(solution)/shard_map/while/body/eval_jaxpr/ppermute | solution.py:10
  701.2 43.1 %collective-permute-done = bf16[128,512]{1,0:T(8,128)(2,1)S(1)} collective-permute-done((bf16[128,512]{1,0:T(8,128)(2,1)S(1)}, bf16[128,512]{1,0:T(8,128)(2,1)S(1)}, u32[]{:S(2)}, u32[]{:S(2)}) %collective-permute-start) | collective-permute-done | bytes 131104 | tf_op jit(solution)/shard_map/while/body/eval_jaxpr/ppermute | solution.py:10
  748.1 24.4 %collective-permute-done = bf16[128,512]{1,0:T(8,128)(2,1)S(1)} collective-permute-done((bf16[128,512]{1,0:T(8,128)(2,1)S(1)}, bf16[128,512]{1,0:T(8,128)(2,1)S(1)}, u32[]{:S(2)}, u32[]{:S(2)}) %collective-permute-start) | collective-permute-done | bytes 131104 | tf_op jit(solution)/shard_map/while/body/eval_jaxpr/ppermute | solution.py:10
  784.6 16.0 collective-permute-done
  812.7 16.0 collective-permute-done
  828.7 17.9 while.67
  865.1 19.9 %collective-permute-done = bf16[128,512]{1,0:T(8,128)(2,1)S(1)} collective-permute-done((bf16[128,512]{1,0:T(8,128)(2,1)S(1)}, bf16[128,512]{1,0:T(8,128)(2,1)S(1)}, u32[]{:S(2)}, u32[]{:S(2)}) %collective-permute-start) | collective-permute-done | bytes 131104 | tf_op jit(solution)/shard_map/while/body/eval_jaxpr/ppermute | solution.py:10
  904.8 17.9 while.67
  956.6 16.0 collective-permute-done
  998.2 26.4 %collective-permute-done = bf16[128,512]{1,0:T(8,128)(2,1)S(1)} collective-permute-done((bf16[128,512]{1,0:T(8,128)(2,1)S(1)}, bf16[128,512]{1,0:T(8,128)(2,1)S(1)}, u32[]{:S(2)}, u32[]{:S(2)}) %collective-permute-start) | collective-permute-done | bytes 131104 | tf_op jit(solution)/shard_map/while/body/eval_jaxpr/ppermute | solution.py:10
  1024.6 17.9 while.67
  1046.4 17.9 while.67
  1082.8 21.9 %collective-permute-done = bf16[128,512]{1,0:T(8,128)(2,1)S(1)} collective-permute-done((bf16[128,512]{1,0:T(8,128)(2,1)S(1)}, bf16[128,512]{1,0:T(8,128)(2,1)S(1)}, u32[]{:S(2)}, u32[]{:S(2)}) %collective-permute-start) | collective-permute-done | bytes 131104 | tf_op jit(solution)/shard_map/while/body/eval_jaxpr/ppermute | solution.py:10
  1108.5 24.4 %collective-permute-done = bf16[128,512]{1,0:T(8,128)(2,1)S(1)} collective-permute-done((bf16[128,512]{1,0:T(8,128)(2,1)S(1)}, bf16[128,512]{1,0:T(8,128)(2,1)S(1)}, u32[]{:S(2)}, u32[]{:S(2)}) %collective-permute-start) | collective-permute-done | bytes 131104 | tf_op jit(solution)/shard_map/while/body/eval_jaxpr/ppermute | solution.py:10
  1221.9 26.4 %collective-permute-done = bf16[128,512]{1,0:T(8,128)(2,1)S(1)} collective-permute-done((bf16[128,512]{1,0:T(8,128)(2,1)S(1)}, bf16[128,512]{1,0:T(8,128)(2,1)S(1)}, u32[]{:S(2)}, u32[]{:S(2)}) %collective-permute-start) | collective-permute-done | bytes 131104 | tf_op jit(solution)/shard_map/while/body/eval_jaxpr/ppermute | solution.py:10
  1252.1 24.4 %collective-permute-done = bf16[128,512]{1,0:T(8,128)(2,1)S(1)} collective-permute-done((bf16[128,512]{1,0:T(8,128)(2,1)S(1)}, bf16[128,512]{1,0:T(8,128)(2,1)S(1)}, u32[]{:S(2)}, u32[]{:S(2)}) %collective-permute-start) | collective-permute-done | bytes 131104 | tf_op jit(solution)/shard_map/while/body/eval_jaxpr/ppermute | solution.py:10
  1276.4 17.9 while.67
  1296.9 18.0 collective-permute-done
  1318.8 24.4 %collective-permute-done = bf16[128,512]{1,0:T(8,128)(2,1)S(1)} collective-permute-done((bf16[128,512]{1,0:T(8,128)(2,1)S(1)}, bf16[128,512]{1,0:T(8,128)(2,1)S(1)}, u32[]{:S(2)}, u32[]{:S(2)}) %collective-permute-start) | collective-permute-done | bytes 131104 | tf_op jit(solution)/shard_map/while/body/eval_jaxpr/ppermute | solution.py:10
  1355.3 16.0 collective-permute-done
  1383.4 16.0 collective-permute-done
  1399.4 17.9 while.67
  1451.2 34.7 %collective-permute-done = bf16[128,512]{1,0:T(8,128)(2,1)S(1)} collective-permute-done((bf16[128,512]{1,0:T(8,128)(2,1)S(1)}, bf16[128,512]{1,0:T(8,128)(2,1)S(1)}, u32[]{:S(2)}, u32[]{:S(2)}) %collective-permute-start) | collective-permute-done | bytes 131104 | tf_op jit(solution)/shard_map/while/body/eval_jaxpr/ppermute | solution.py:10
  1489.7 34.7 %collective-permute-done = bf16[128,512]{1,0:T(8,128)(2,1)S(1)} collective-permute-done((bf16[128,512]{1,0:T(8,128)(2,1)S(1)}, bf16[128,512]{1,0:T(8,128)(2,1)S(1)}, u32[]{:S(2)}, u32[]{:S(2)}) %collective-permute-start) | collective-permute-done | bytes 131104 | tf_op jit(solution)/shard_map/while/body/eval_jaxpr/ppermute | solution.py:10
  1528.2 24.4 %collective-permute-done = bf16[128,512]{1,0:T(8,128)(2,1)S(1)} collective-permute-done((bf16[128,512]{1,0:T(8,128)(2,1)S(1)}, bf16[128,512]{1,0:T(8,128)(2,1)S(1)}, u32[]{:S(2)}, u32[]{:S(2)}) %collective-permute-start) | collective-permute-done | bytes 131104 | tf_op jit(solution)/shard_map/while/body/eval_jaxpr/ppermute | solution.py:10
  1605.5 38.7 %collective-permute-done = bf16[128,512]{1,0:T(8,128)(2,1)S(1)} collective-permute-done((bf16[128,512]{1,0:T(8,128)(2,1)S(1)}, bf16[128,512]{1,0:T(8,128)(2,1)S(1)}, u32[]{:S(2)}, u32[]{:S(2)}) %collective-permute-start) | collective-permute-done | bytes 131104 | tf_op jit(solution)/shard_map/while/body/eval_jaxpr/ppermute | solution.py:10
  1648.0 24.4 %collective-permute-done = bf16[128,512]{1,0:T(8,128)(2,1)S(1)} collective-permute-done((bf16[128,512]{1,0:T(8,128)(2,1)S(1)}, bf16[128,512]{1,0:T(8,128)(2,1)S(1)}, u32[]{:S(2)}, u32[]{:S(2)}) %collective-permute-start) | collective-permute-done | bytes 131104 | tf_op jit(solution)/shard_map/while/body/eval_jaxpr/ppermute | solution.py:10
  1676.1 24.4 %collective-permute-done = bf16[128,512]{1,0:T(8,128)(2,1)S(1)} collective-permute-done((bf16[128,512]{1,0:T(8,128)(2,1)S(1)}, bf16[128,512]{1,0:T(8,128)(2,1)S(1)}, u32[]{:S(2)}, u32[]{:S(2)}) %collective-permute-start) | collective-permute-done | bytes 131104 | tf_op jit(solution)/shard_map/while/body/eval_jaxpr/ppermute | solution.py:10
  1726.1 24.4 %collective-permute-done = bf16[128,512]{1,0:T(8,128)(2,1)S(1)} collective-permute-done((bf16[128,512]{1,0:T(8,128)(2,1)S(1)}, bf16[128,512]{1,0:T(8,128)(2,1)S(1)}, u32[]{:S(2)}, u32[]{:S(2)}) %collective-permute-start) | collective-permute-done | bytes 131104 | tf_op jit(solution)/shard_map/while/body/eval_jaxpr/ppermute | solution.py:10
  1789.4 137.5 %reduce-scatter.2.cloned.1.call-done = bf16[128,512]{1,0:T(8,128)(2,1)} async-done(((bf16[1024,512]{1,0:T(8,128)(2,1)}), bf16[128,512]{1,0:T(8,128)(2,1)}) %reduce-scatter.2.cloned.1.call-update) | async-done | bytes 131088 | tf_op jit(solution)/shard_map/reduce_scatter | solution.py:62
  (388 shorter events, 794.7 us)
Async XLA Ops:
  6.5 75.2 %all-gather.2.cloned.1.call-start = ((), (), s32[]{:S(2)}) async-start(), calls=%async_computation.1 | async-start | bytes 1179648 | tf_op jit(solution)/shard_map/all_gather | solution.py:20
  9.4 1917.5 %reduce-scatter.2.cloned.1.call-start = ((), (), s32[]{:S(2)}) async-start(), calls=%async_computation.2 | async-start | bytes 1179648 | tf_op jit(solution)/shard_map/reduce_scatter | solution.py:62
  83.2 23.3 %collective-permute-start = (bf16[128,512]{1,0:T(8,128)(2,1)S(1)}, bf16[128,512]{1,0:T(8,128)(2,1)S(1)}, u32[]{:S(2)}, u32[]{:S(2)}) collective-permute-start(bf16[128,512]{1,0:T(8,128)(2,1)S(1)} %get-tuple-element.784), channel_id=1, source_target_pairs={{504,0},{0,8},{8,16},{16,24},{24,32},{32,40},{40,48},{48,56},{56,6... | collective-permute-start | bytes 393224 | tf_op jit(solution)/shard_map/while/body/eval_jaxpr/ppermute | solution.py:10
  116.2 25.7 %collective-permute-start = (bf16[128,512]{1,0:T(8,128)(2,1)S(1)}, bf16[128,512]{1,0:T(8,128)(2,1)S(1)}, u32[]{:S(2)}, u32[]{:S(2)}) collective-permute-start(bf16[128,512]{1,0:T(8,128)(2,1)S(1)} %get-tuple-element.784), channel_id=1, source_target_pairs={{504,0},{0,8},{8,16},{16,24},{24,32},{32,40},{40,48},{48,56},{56,6... | collective-permute-start | bytes 393224 | tf_op jit(solution)/shard_map/while/body/eval_jaxpr/ppermute | solution.py:10
  151.5 18.6 collective-permute-start
  171.3 18.5 collective-permute-start
  191.1 37.3 %collective-permute-start = (bf16[128,512]{1,0:T(8,128)(2,1)S(1)}, bf16[128,512]{1,0:T(8,128)(2,1)S(1)}, u32[]{:S(2)}, u32[]{:S(2)}) collective-permute-start(bf16[128,512]{1,0:T(8,128)(2,1)S(1)} %get-tuple-element.784), channel_id=1, source_target_pairs={{504,0},{0,8},{8,16},{16,24},{24,32},{32,40},{40,48},{48,56},{56,6... | collective-permute-start | bytes 393224 | tf_op jit(solution)/shard_map/while/body/eval_jaxpr/ppermute | solution.py:10
  229.6 26.9 %collective-permute-start = (bf16[128,512]{1,0:T(8,128)(2,1)S(1)}, bf16[128,512]{1,0:T(8,128)(2,1)S(1)}, u32[]{:S(2)}, u32[]{:S(2)}) collective-permute-start(bf16[128,512]{1,0:T(8,128)(2,1)S(1)} %get-tuple-element.784), channel_id=1, source_target_pairs={{504,0},{0,8},{8,16},{16,24},{24,32},{32,40},{40,48},{48,56},{56,6... | collective-permute-start | bytes 393224 | tf_op jit(solution)/shard_map/while/body/eval_jaxpr/ppermute | solution.py:10
  266.1 18.5 collective-permute-start
  302.6 18.6 collective-permute-start
  322.4 18.5 collective-permute-start
  350.6 18.5 collective-permute-start
  390.2 26.9 %collective-permute-start = (bf16[128,512]{1,0:T(8,128)(2,1)S(1)}, bf16[128,512]{1,0:T(8,128)(2,1)S(1)}, u32[]{:S(2)}, u32[]{:S(2)}) collective-permute-start(bf16[128,512]{1,0:T(8,128)(2,1)S(1)} %get-tuple-element.784), channel_id=1, source_target_pairs={{504,0},{0,8},{8,16},{16,24},{24,32},{32,40},{40,48},{48,56},{56,6... | collective-permute-start | bytes 393224 | tf_op jit(solution)/shard_map/while/body/eval_jaxpr/ppermute | solution.py:10
  468.3 26.9 %collective-permute-start = (bf16[128,512]{1,0:T(8,128)(2,1)S(1)}, bf16[128,512]{1,0:T(8,128)(2,1)S(1)}, u32[]{:S(2)}, u32[]{:S(2)}) collective-permute-start(bf16[128,512]{1,0:T(8,128)(2,1)S(1)} %get-tuple-element.784), channel_id=1, source_target_pairs={{504,0},{0,8},{8,16},{16,24},{24,32},{32,40},{40,48},{48,56},{56,6... | collective-permute-start | bytes 393224 | tf_op jit(solution)/shard_map/while/body/eval_jaxpr/ppermute | solution.py:10
  509.9 26.9 %collective-permute-start = (bf16[128,512]{1,0:T(8,128)(2,1)S(1)}, bf16[128,512]{1,0:T(8,128)(2,1)S(1)}, u32[]{:S(2)}, u32[]{:S(2)}) collective-permute-start(bf16[128,512]{1,0:T(8,128)(2,1)S(1)} %get-tuple-element.784), channel_id=1, source_target_pairs={{504,0},{0,8},{8,16},{16,24},{24,32},{32,40},{40,48},{48,56},{56,6... | collective-permute-start | bytes 393224 | tf_op jit(solution)/shard_map/while/body/eval_jaxpr/ppermute | solution.py:10
  538.1 18.5 collective-permute-start
  586.0 35.3 %collective-permute-start = (bf16[128,512]{1,0:T(8,128)(2,1)S(1)}, bf16[128,512]{1,0:T(8,128)(2,1)S(1)}, u32[]{:S(2)}, u32[]{:S(2)}) collective-permute-start(bf16[128,512]{1,0:T(8,128)(2,1)S(1)} %get-tuple-element.784), channel_id=1, source_target_pairs={{504,0},{0,8},{8,16},{16,24},{24,32},{32,40},{40,48},{48,56},{56,6... | collective-permute-start | bytes 393224 | tf_op jit(solution)/shard_map/while/body/eval_jaxpr/ppermute | solution.py:10
  630.9 18.6 collective-permute-start
  662.1 26.9 %collective-permute-start = (bf16[128,512]{1,0:T(8,128)(2,1)S(1)}, bf16[128,512]{1,0:T(8,128)(2,1)S(1)}, u32[]{:S(2)}, u32[]{:S(2)}) collective-permute-start(bf16[128,512]{1,0:T(8,128)(2,1)S(1)} %get-tuple-element.784), channel_id=1, source_target_pairs={{504,0},{0,8},{8,16},{16,24},{24,32},{32,40},{40,48},{48,56},{56,6... | collective-permute-start | bytes 393224 | tf_op jit(solution)/shard_map/while/body/eval_jaxpr/ppermute | solution.py:10
  698.6 45.6 %collective-permute-start = (bf16[128,512]{1,0:T(8,128)(2,1)S(1)}, bf16[128,512]{1,0:T(8,128)(2,1)S(1)}, u32[]{:S(2)}, u32[]{:S(2)}) collective-permute-start(bf16[128,512]{1,0:T(8,128)(2,1)S(1)} %get-tuple-element.784), channel_id=1, source_target_pairs={{504,0},{0,8},{8,16},{16,24},{24,32},{32,40},{40,48},{48,56},{56,6... | collective-permute-start | bytes 393224 | tf_op jit(solution)/shard_map/while/body/eval_jaxpr/ppermute | solution.py:10
  745.5 26.9 %collective-permute-start = (bf16[128,512]{1,0:T(8,128)(2,1)S(1)}, bf16[128,512]{1,0:T(8,128)(2,1)S(1)}, u32[]{:S(2)}, u32[]{:S(2)}) collective-permute-start(bf16[128,512]{1,0:T(8,128)(2,1)S(1)} %get-tuple-element.784), channel_id=1, source_target_pairs={{504,0},{0,8},{8,16},{16,24},{24,32},{32,40},{40,48},{48,56},{56,6... | collective-permute-start | bytes 393224 | tf_op jit(solution)/shard_map/while/body/eval_jaxpr/ppermute | solution.py:10
  782.0 18.5 collective-permute-start
  810.2 18.6 collective-permute-start
  860.2 24.9 %collective-permute-start = (bf16[128,512]{1,0:T(8,128)(2,1)S(1)}, bf16[128,512]{1,0:T(8,128)(2,1)S(1)}, u32[]{:S(2)}, u32[]{:S(2)}) collective-permute-start(bf16[128,512]{1,0:T(8,128)(2,1)S(1)} %get-tuple-element.784), channel_id=1, source_target_pairs={{504,0},{0,8},{8,16},{16,24},{24,32},{32,40},{40,48},{48,56},{56,6... | collective-permute-start | bytes 393224 | tf_op jit(solution)/shard_map/while/body/eval_jaxpr/ppermute | solution.py:10
  894.6 10.2 collective-permute-start
  954.0 18.5 collective-permute-start
  982.2 12.2 collective-permute-start
  995.7 28.9 %collective-permute-start = (bf16[128,512]{1,0:T(8,128)(2,1)S(1)}, bf16[128,512]{1,0:T(8,128)(2,1)S(1)}, u32[]{:S(2)}, u32[]{:S(2)}) collective-permute-start(bf16[128,512]{1,0:T(8,128)(2,1)S(1)} %get-tuple-element.784), channel_id=1, source_target_pairs={{504,0},{0,8},{8,16},{16,24},{24,32},{32,40},{40,48},{48,56},{56,6... | collective-permute-start | bytes 393224 | tf_op jit(solution)/shard_map/while/body/eval_jaxpr/ppermute | solution.py:10
  1075.8 28.9 %collective-permute-start = (bf16[128,512]{1,0:T(8,128)(2,1)S(1)}, bf16[128,512]{1,0:T(8,128)(2,1)S(1)}, u32[]{:S(2)}, u32[]{:S(2)}) collective-permute-start(bf16[128,512]{1,0:T(8,128)(2,1)S(1)} %get-tuple-element.784), channel_id=1, source_target_pairs={{504,0},{0,8},{8,16},{16,24},{24,32},{32,40},{40,48},{48,56},{56,6... | collective-permute-start | bytes 393224 | tf_op jit(solution)/shard_map/while/body/eval_jaxpr/ppermute | solution.py:10
  1106.0 26.9 %collective-permute-start = (bf16[128,512]{1,0:T(8,128)(2,1)S(1)}, bf16[128,512]{1,0:T(8,128)(2,1)S(1)}, u32[]{:S(2)}, u32[]{:S(2)}) collective-permute-start(bf16[128,512]{1,0:T(8,128)(2,1)S(1)} %get-tuple-element.784), channel_id=1, source_target_pairs={{504,0},{0,8},{8,16},{16,24},{24,32},{32,40},{40,48},{48,56},{56,6... | collective-permute-start | bytes 393224 | tf_op jit(solution)/shard_map/while/body/eval_jaxpr/ppermute | solution.py:10
  1142.5 12.2 collective-permute-start
  1164.3 12.2 collective-permute-start
  1191.2 18.5 collective-permute-start
  1219.4 28.9 %collective-permute-start = (bf16[128,512]{1,0:T(8,128)(2,1)S(1)}, bf16[128,512]{1,0:T(8,128)(2,1)S(1)}, u32[]{:S(2)}, u32[]{:S(2)}) collective-permute-start(bf16[128,512]{1,0:T(8,128)(2,1)S(1)} %get-tuple-element.784), channel_id=1, source_target_pairs={{504,0},{0,8},{8,16},{16,24},{24,32},{32,40},{40,48},{48,56},{56,6... | collective-permute-start | bytes 393224 | tf_op jit(solution)/shard_map/while/body/eval_jaxpr/ppermute | solution.py:10
  1249.5 26.9 %collective-permute-start = (bf16[128,512]{1,0:T(8,128)(2,1)S(1)}, bf16[128,512]{1,0:T(8,128)(2,1)S(1)}, u32[]{:S(2)}, u32[]{:S(2)}) collective-permute-start(bf16[128,512]{1,0:T(8,128)(2,1)S(1)} %get-tuple-element.784), channel_id=1, source_target_pairs={{504,0},{0,8},{8,16},{16,24},{24,32},{32,40},{40,48},{48,56},{56,6... | collective-permute-start | bytes 393224 | tf_op jit(solution)/shard_map/while/body/eval_jaxpr/ppermute | solution.py:10
  1294.4 20.6 %collective-permute-start = (bf16[128,512]{1,0:T(8,128)(2,1)S(1)}, bf16[128,512]{1,0:T(8,128)(2,1)S(1)}, u32[]{:S(2)}, u32[]{:S(2)}) collective-permute-start(bf16[128,512]{1,0:T(8,128)(2,1)S(1)} %get-tuple-element.784), channel_id=1, source_target_pairs={{504,0},{0,8},{8,16},{16,24},{24,32},{32,40},{40,48},{48,56},{56,6... | collective-permute-start | bytes 393224 | tf_op jit(solution)/shard_map/while/body/eval_jaxpr/ppermute | solution.py:10
  1316.2 26.9 %collective-permute-start = (bf16[128,512]{1,0:T(8,128)(2,1)S(1)}, bf16[128,512]{1,0:T(8,128)(2,1)S(1)}, u32[]{:S(2)}, u32[]{:S(2)}) collective-permute-start(bf16[128,512]{1,0:T(8,128)(2,1)S(1)} %get-tuple-element.784), channel_id=1, source_target_pairs={{504,0},{0,8},{8,16},{16,24},{24,32},{32,40},{40,48},{48,56},{56,6... | collective-permute-start | bytes 393224 | tf_op jit(solution)/shard_map/while/body/eval_jaxpr/ppermute | solution.py:10
  1352.7 18.5 collective-permute-start
  1380.9 18.5 collective-permute-start
  1417.4 10.2 collective-permute-start
  1448.6 37.3 %collective-permute-start = (bf16[128,512]{1,0:T(8,128)(2,1)S(1)}, bf16[128,512]{1,0:T(8,128)(2,1)S(1)}, u32[]{:S(2)}, u32[]{:S(2)}) collective-permute-start(bf16[128,512]{1,0:T(8,128)(2,1)S(1)} %get-tuple-element.784), channel_id=1, source_target_pairs={{504,0},{0,8},{8,16},{16,24},{24,32},{32,40},{40,48},{48,56},{56,6... | collective-permute-start | bytes 393224 | tf_op jit(solution)/shard_map/while/body/eval_jaxpr/ppermute | solution.py:10
  1487.2 37.3 %collective-permute-start = (bf16[128,512]{1,0:T(8,128)(2,1)S(1)}, bf16[128,512]{1,0:T(8,128)(2,1)S(1)}, u32[]{:S(2)}, u32[]{:S(2)}) collective-permute-start(bf16[128,512]{1,0:T(8,128)(2,1)S(1)} %get-tuple-element.784), channel_id=1, source_target_pairs={{504,0},{0,8},{8,16},{16,24},{24,32},{32,40},{40,48},{48,56},{56,6... | collective-permute-start | bytes 393224 | tf_op jit(solution)/shard_map/while/body/eval_jaxpr/ppermute | solution.py:10
  1525.7 26.9 %collective-permute-start = (bf16[128,512]{1,0:T(8,128)(2,1)S(1)}, bf16[128,512]{1,0:T(8,128)(2,1)S(1)}, u32[]{:S(2)}, u32[]{:S(2)}) collective-permute-start(bf16[128,512]{1,0:T(8,128)(2,1)S(1)} %get-tuple-element.784), channel_id=1, source_target_pairs={{504,0},{0,8},{8,16},{16,24},{24,32},{32,40},{40,48},{48,56},{56,6... | collective-permute-start | bytes 393224 | tf_op jit(solution)/shard_map/while/body/eval_jaxpr/ppermute | solution.py:10
  1598.5 45.6 %collective-permute-start = (bf16[128,512]{1,0:T(8,128)(2,1)S(1)}, bf16[128,512]{1,0:T(8,128)(2,1)S(1)}, u32[]{:S(2)}, u32[]{:S(2)}) collective-permute-start(bf16[128,512]{1,0:T(8,128)(2,1)S(1)} %get-tuple-element.784), channel_id=1, source_target_pairs={{504,0},{0,8},{8,16},{16,24},{24,32},{32,40},{40,48},{48,56},{56,6... | collective-permute-start | bytes 393224 | tf_op jit(solution)/shard_map/while/body/eval_jaxpr/ppermute | solution.py:10
  1645.4 26.9 %collective-permute-start = (bf16[128,512]{1,0:T(8,128)(2,1)S(1)}, bf16[128,512]{1,0:T(8,128)(2,1)S(1)}, u32[]{:S(2)}, u32[]{:S(2)}) collective-permute-start(bf16[128,512]{1,0:T(8,128)(2,1)S(1)} %get-tuple-element.784), channel_id=1, source_target_pairs={{504,0},{0,8},{8,16},{16,24},{24,32},{32,40},{40,48},{48,56},{56,6... | collective-permute-start | bytes 393224 | tf_op jit(solution)/shard_map/while/body/eval_jaxpr/ppermute | solution.py:10
  1673.6 26.9 %collective-permute-start = (bf16[128,512]{1,0:T(8,128)(2,1)S(1)}, bf16[128,512]{1,0:T(8,128)(2,1)S(1)}, u32[]{:S(2)}, u32[]{:S(2)}) collective-permute-start(bf16[128,512]{1,0:T(8,128)(2,1)S(1)} %get-tuple-element.784), channel_id=1, source_target_pairs={{504,0},{0,8},{8,16},{16,24},{24,32},{32,40},{40,48},{48,56},{56,6... | collective-permute-start | bytes 393224 | tf_op jit(solution)/shard_map/while/body/eval_jaxpr/ppermute | solution.py:10
  1723.5 26.9 %collective-permute-start = (bf16[128,512]{1,0:T(8,128)(2,1)S(1)}, bf16[128,512]{1,0:T(8,128)(2,1)S(1)}, u32[]{:S(2)}, u32[]{:S(2)}) collective-permute-start(bf16[128,512]{1,0:T(8,128)(2,1)S(1)} %get-tuple-element.784), channel_id=1, source_target_pairs={{504,0},{0,8},{8,16},{16,24},{24,32},{32,40},{40,48},{48,56},{56,6... | collective-permute-start | bytes 393224 | tf_op jit(solution)/shard_map/while/body/eval_jaxpr/ppermute | solution.py:10
  1760.1 18.5 collective-permute-start
  (21 other events, 474.4 us)
Sparse Core Ops, SparseCore 0:
  10.5 71.1 all-gather.1
  1789.5 137.3 reduce-scatter.1
where the time goes:
time: 1950 us; the launch traced here: 1940 us
  waiting for transfers between devices  1230 us (63%)
  loops' own time  388 us (20%)
  starting transfers between devices  166 us (9%)
  local copies, waits for them, and re-layouts  71.6 us (4%)
  matrix products  66.6 us (3%)
    ppermute x63, waiting for transfers between devices, from_behind(): return lax.ppermute(block, axis, route)  1020 us
    another operation x64, loops' own time, one_step(): lax.fori_loop(bounds[step_num], bounds[step_num + 1], lambda tile_num, ac...  385 us
    ppermute x63, starting transfers between devices, from_behind(): return lax.ppermute(block, axis, route)  166 us
    reduce_scatter x1, waiting for transfers between devices, on_device(): lax.psum_scatter(partial_value.astype(jnp.bfloat16), 'rep', scatter_dimen...  138 us
    all_gather x1, waiting for transfers between devices, on_device(): receivers = lax.all_gather(query_rows, 'rep', axis=0, tiled=True)  68.9 us
    dot_general x48, matrix products, one_tile(): contrib = jnp.dot(weighted, sender, preferred_element_type=jnp.float32)  61.7 us
  transfers between devices with their start and end apart: 65, of which 65 were waited for; matrix products, arithmetic and copies ran while one was open for 2% of the time, Pallas kernels for 0%

commit v1 on v0

v1 whole, which is shorter than its diff:
```python
import jax
import jax.numpy as jnp
from jax import lax
from jax.experimental import pallas as pl
from jax.experimental.pallas import tpu as pltpu
from jax.sharding import PartitionSpec as P

F32 = jnp.float32
BF16 = jnp.bfloat16


def tiles_kernel(slot_ref, count_ref, query_ref, source_ref, weight_ref, out_ref, total):
    n_rep, _, width = query_ref.shape
    factor = 1.0 / float(width) ** 0.5
    total[...] = jnp.zeros_like(total)

    def one_tile(t, carry):
        slot = slot_ref[t]
        row = lax.rem(slot, n_rep)
        step = lax.div(slot, n_rep)
        source = source_ref[step]
        scores = lax.dot_general(
            query_ref[row], source, (((1,), (1,)), ((), ())), preferred_element_type=F32
        )
        weighted = (jnp.tanh(scores * factor) * weight_ref[t].astype(F32)).astype(BF16)
        total[row] += jnp.dot(weighted, source, preferred_element_type=F32)
        return carry

    lax.fori_loop(0, count_ref[0], one_tile, 0)
    out_ref[...] = total[...].astype(BF16)


def on_device(features, w_query, w_key, w_out, edge_weight, tile_slot, tile_count):
    rows, width = features.shape
    n_wide = lax.axis_size("wide")
    n_rep = lax.axis_size("rep")
    query_rows = jnp.dot(features, w_query, preferred_element_type=F32).astype(BF16)
    key_rows = jnp.dot(features, w_key, preferred_element_type=F32).astype(BF16)
    sources = lax.all_gather(key_rows, "wide", axis=0)
    receivers = lax.all_gather(query_rows, "rep", axis=0)
    slots = tile_slot[0, 0]
    me = lax.axis_index("wide")
    slots = (me - slots // n_rep) % n_wide * n_rep + slots % n_rep
    partial = pl.pallas_call(
        tiles_kernel,
        out_shape=jax.ShapeDtypeStruct((n_rep, rows, width), BF16),
        in_specs=[pl.BlockSpec(memory_space=pltpu.SMEM)] * 2
        + [pl.BlockSpec(memory_space=pltpu.VMEM)] * 3,
        out_specs=pl.BlockSpec(memory_space=pltpu.VMEM),
        scratch_shapes=[pltpu.VMEM((n_rep, rows, width), F32)],
        compiler_params=pltpu.CompilerParams(vmem_limit_bytes=40 * 2**20),
    )(slots, tile_count[0], receivers, sources, edge_weight[0, 0])
    summed = lax.psum_scatter(
        partial.reshape(n_rep * rows, width), "rep", scatter_dimension=0, tiled=True
    )
    mixed = features.astype(F32) + jnp.dot(summed, w_out, preferred_element_type=F32)
    return mixed.astype(BF16)


def solution(mesh):
    in_specs = (
        P(("wide", "rep"), None),
        P(),
        P(),
        P(),
        P("wide", "rep", None, None, None),
        P("wide", "rep", None),
        P("wide", "rep"),
    )
    out_specs = P(("wide", "rep"), None)
    return jax.shard_map(
        on_device, mesh=mesh, in_specs=in_specs, out_specs=out_specs, check_vma=False
    )
```

time: 1950 us -> 350 us (0.18)
  waiting for transfers between devices: 1230 us -> 283 us
  loops' own time: 388 us -> 0 us
  starting transfers between devices: 166 us -> 0.09 us
  local copies, waits for them, and re-layouts: 71.6 us -> 7.53 us
  matrix products: 66.6 us -> 5.59 us
  Pallas kernels: 0 us -> 38.1 us
    ppermute x63 -> x0, waiting for transfers between devices: 1020 us -> none  [from_behind(): return lax.ppermute(block, axis, route)]
    another operation x65 -> x0, loops' own time: 388 us -> none  [the longest x64 385 us: one_step(): lax.fori_loop(bounds[step_num], bounds[step_num + 1], lambda tile_num, ac...]
    ppermute x63 -> x0, starting transfers between devices: 166 us -> none  [from_behind(): return lax.ppermute(block, axis, route)]
    all_gather x1 -> x2, waiting for transfers between devices: 68.9 us -> 194 us  [the longest x1 125 us: on_device(): sources = lax.all_gather(key_rows, 'wide', axis=0)]
    dynamic_slice x111 -> x0, local copies, waits for them, and re-layouts: 69.1 us -> none  [the longest x63 37.3 us: one_step(): bounds[step_num + 1]]
    dot_general x51 -> x3, matrix products: 66.6 us -> 5.59 us  [the longest x1 2.01 us: on_device(): key_rows = jnp.dot(features, w_key, preferred_element_type=F32).astype(BF16)]
    reduce_scatter x1, waiting for transfers between devices: 138 us -> 89.5 us  [on_device(): lax.psum_scatter(partial.reshape(n_rep * rows, width), 'rep', scatter_dim...]
    pallas_call x0 -> x1, Pallas kernels: none -> 38.1 us  [on_device(): pl.pallas_call(tiles_kernel, out_shape=jax.ShapeDtypeStruct((n_rep, rows,...]
  transfers between devices with their start and end apart: 65 -> 3, of which waited for: 65 -> 3; matrix products, arithmetic and copies ran while one was open for 2% -> 1% of each run, Pallas kernels for 0% -> 0%
where the time goes in v1:
time: 350 us; the launch traced here: 349 us
  waiting for transfers between devices  283 us (81%)
  Pallas kernels  38.1 us (11%)
  between operations  13.8 us (4%)
  local copies, waits for them, and re-layouts  7.53 us (2%)
  matrix products  5.59 us (2%)
    all_gather x1, waiting for transfers between devices, on_device(): sources = lax.all_gather(key_rows, 'wide', axis=0)  125 us
    reduce_scatter x1, waiting for transfers between devices, on_device(): lax.psum_scatter(partial.reshape(n_rep * rows, width), 'rep', scatter_dim...  89.5 us
    all_gather x1, waiting for transfers between devices, on_device(): receivers = lax.all_gather(query_rows, 'rep', axis=0)  68.8 us
    pallas_call x1, Pallas kernels, on_device(): pl.pallas_call(tiles_kernel, out_shape=jax.ShapeDtypeStruct((n_rep, rows,...  38.1 us
    unnamed x12, local copies, waits for them, and re-layouts  7.53 us
  transfers between devices with their start and end apart: 3, of which 3 were waited for; matrix products, arithmetic and copies ran while one was open for 1% of the time, Pallas kernels for 0%

profile of v1, /device:TPU:1, one launch (start us, length us, event | category | flops | bytes accessed | tf_op | source)
XLA Modules:
  0.0 349.0 jit_solution(16813976015570215731)
XLA Ops:
  6.5 0.0 copy-start
  6.5 0.0 copy-start.4
  6.5 0.0 copy-start.5
  6.5 0.0 all-gather.5.cloned.1.call-start
  6.5 1.0 copy-done
  7.6 1.8 convolution_convert_fusion.1
  9.4 0.0 all-gather.5.cloned.1.call-update
  9.4 0.0 all-gather.7.cloned.1.call-start
  9.4 2.0 convolution_convert_fusion
  11.5 0.0 all-gather.7.cloned.1.call-update
  11.5 0.0 reduce-scatter.2.cloned.1.call-start
  12.2 0.7 fusion.1.slot_ref
  12.9 68.8 %all-gather.5.cloned.1.call-done = bf16[1024,512]{1,0:T(8,128)(2,1)} async-done(((bf16[128,512]{1,0:T(8,128)(2,1)}), bf16[1024,512]{1,0:T(8,128)(2,1)}) %all-gather.5.cloned.1.call-update) | async-done | bytes 1048592 | tf_op jit(solution)/shard_map/all_gather | solution.py:40
  81.7 124.9 %all-gather.7.cloned.1.call-done = bf16[8192,512]{1,0:T(8,128)(2,1)} async-done(((bf16[128,512]{1,0:T(8,128)(2,1)}), bf16[8192,512]{1,0:T(8,128)(2,1)}) %all-gather.7.cloned.1.call-update) | async-done | bytes 8388624 | tf_op jit(solution)/shard_map/all_gather | solution.py:39
  206.6 0.0 copy-start.1
  206.6 3.4 copy-done.1
  210.0 0.0 copy-start.2
  210.0 1.9 copy-done.2
  211.9 0.0 copy-start.3
  211.9 1.2 copy-done.3
  213.1 38.1 %shard_map.73 = bf16[8,128,512]{2,1,0:T(8,128)(2,1)} custom-call(s32[96]{0:T(128)S(1)} %fusion.1.slot_ref, s32[1]{0:T(128)} %bitcast.24.count_ref, bf16[8,128,512]{2,1,0:T(8,128)(2,1)S(1)} %bitcast.27, bf16[64,128,512]{2,1,0:T(8,128)(2,1)S(1)} %bitcast.25, bf16[96,128,128]{2,1,0:T(8,128)(2,1)S(1)} %bitcast.26), custom_call_target="tpu_custom_call" | custom-call | tf_op jit(solution)/shard_map/pallas_call | solution.py:44
  251.1 0.0 reduce-scatter.2.cloned.1.call-update
  251.2 89.5 %reduce-scatter.2.cloned.1.call-done = bf16[128,512]{1,0:T(8,128)(2,1)} async-done(((bf16[1024,512]{1,0:T(8,128)(2,1)}), bf16[128,512]{1,0:T(8,128)(2,1)}) %reduce-scatter.2.cloned.1.call-update) | async-done | bytes 131088 | tf_op jit(solution)/shard_map/reduce_scatter | solution.py:53
  340.6 0.0 copy-done.4
  340.6 0.0 copy-done.5
  340.6 1.8 fusion
Async XLA Ops:
  6.5 1.0 copy-start
  6.5 334.1 %copy-start.4 = (bf16[128,512]{1,0:T(8,128)(2,1)S(1)}, bf16[128,512]{1,0:T(8,128)(2,1)}, u32[]{:S(2)}) copy-start(bf16[128,512]{1,0:T(8,128)(2,1)} %param.7) | copy-start | bytes 393220
  6.5 334.1 %copy-start.5 = (bf16[512,512]{1,0:T(8,128)(2,1)S(1)}, bf16[512,512]{1,0:T(8,128)(2,1)}, u32[]{:S(2)}) copy-start(bf16[512,512]{1,0:T(8,128)(2,1)} %param.10) | copy-start | bytes 1572868
  6.5 75.2 %all-gather.5.cloned.1.call-start = ((), (), s32[]{:S(2)}) async-start(), calls=%async_computation.2 | async-start | bytes 1179648 | tf_op jit(solution)/shard_map/all_gather | solution.py:40
  9.4 197.2 %all-gather.7.cloned.1.call-start = ((), (), s32[]{:S(2)}) async-start(), calls=%async_computation.3 | async-start | bytes 8519680 | tf_op jit(solution)/shard_map/all_gather | solution.py:39
  11.5 329.1 %reduce-scatter.2.cloned.1.call-start = ((), (), s32[]{:S(2)}) async-start(), calls=%async_computation.1 | async-start | bytes 1179648 | tf_op jit(solution)/shard_map/reduce_scatter | solution.py:53
  206.6 3.4 copy-start.1
  210.0 1.9 copy-start.2
  211.9 1.2 copy-start.3
Sparse Core Ops, SparseCore 0:
  10.5 71.1 all-gather.4
  83.9 122.6 all-gather.6
  251.3 89.2 reduce-scatter.1

commit v2 on v1

v2 whole, which is shorter than its diff:
```python
import functools

import jax
import jax.numpy as jnp
from jax import lax
from jax.experimental import pallas as pl
from jax.experimental.pallas import tpu as pltpu
from jax.sharding import PartitionSpec as P

F32 = jnp.float32
BF16 = jnp.bfloat16
MESH = pl.DeviceIdType.MESH

NY, NZ, NX = 8, 4, 4


def layer_kernel(
    feat, w_query, w_key, w_out, edge, inv, out,
    src, qry, wts, total, pbuf, part, far, near, merged, joined, zbuf,
    recv, send_p, send_s, send_z, send_c, qrecv, qsend, xrecv, xsend, local,
):
    n_wide = src.shape[0]
    rows, width = feat.shape
    n_live = edge.shape[0]
    factor = 1.0 / float(width) ** 0.5
    w, r = lax.axis_index("wide"), lax.axis_index("rep")
    c, zl, y = w % 2, (w // 2) % NZ, w // 8
    zh, x = r // NX, r % NX
    zo = 1 - zh
    sgn = 1 - 2 * c

    def block_of(yy, zz):
        return ((yy + 2 * NY) % NY) * 8 + (zz % NZ) * 2 + c

    def rep_of(zz, xx):
        return zz * NX + (xx + NX) % NX

    ahead = (block_of(y + sgn, zl), r)
    behind = (block_of(y - sgn, zl), r)
    partner = (w + sgn, r)
    z_peers = [(block_of(y, zl + k), r) for k in (1, 2, 3)]
    x_ahead = (w, rep_of(zh, x + sgn))
    x_behind = (w, rep_of(zh, x - sgn))
    z_far = (w, rep_of(zo, x))

    def remote(a, b, s_sem, r_sem, device):
        return pltpu.make_async_remote_copy(
            src_ref=a, dst_ref=b, send_sem=s_sem, recv_sem=r_sem,
            device_id=device, device_id_type=MESH,
        )

    def move(b, s_sem, device):
        return remote(src.at[b], src.at[b], s_sem, recv.at[b], device)

    def qmove(b, k, device):
        return remote(qry.at[b], qry.at[b], qsend.at[k], qrecv.at[b], device)

    barrier = pltpu.get_barrier_semaphore()
    talk = [ahead, behind, partner] + z_peers + [x_ahead, x_behind, z_far]
    for device in talk:
        pl.semaphore_signal(barrier, inc=1, device_id=device, device_id_type=MESH)

    load = pltpu.make_async_copy(edge, wts.at[pl.ds(0, n_live)], local)
    load.start()
    wts[n_live] = jnp.zeros(wts.shape[1:], BF16)
    src[w] = jnp.dot(feat[...], w_key[...], preferred_element_type=F32).astype(BF16)
    qry[r] = jnp.dot(feat[...], w_query[...], preferred_element_type=F32).astype(BF16)
    total[...] = jnp.zeros_like(total)
    pl.semaphore_wait(barrier, len(talk))

    def got(b):
        move(b, send_p.at[0], ahead).wait_recv()

    def qgot(b):
        qmove(b, 0, x_ahead).wait_recv()

    def hold_first(b, k):
        move(b, send_p.at[k], ahead).start()
        move(b, send_s.at[k], behind).start()
        move(b, send_c.at[2 * k], partner).start()

    def event(dd, j):
        if dd == 0:
            b = block_of(y, zl + j)
            got(b)
            hold_first(b, j)
        else:
            b = block_of(y + sgn * dd, zl + j)
            got(b)
            if dd < 3:
                move(b, send_s.at[4 * dd + j], behind).start()
            move(b, send_c.at[2 * (4 * dd + j)], partner).start()
        forward(dd, j)

    def forward(dd, j):
        b = block_of(y - sgn * (dd + 1), zl + j)
        got(b)
        if dd < 3:
            move(b, send_p.at[4 * dd + 4 + j], ahead).start()
        move(b, send_c.at[2 * (4 * dd + j) + 1], partner).start()

    def pair(n):
        m, side = n // 2, n % 2
        dd, j = m // 4, m % 4
        b = block_of(y + sgn * (dd - side * (2 * dd + 1)), zl + j)
        got(b + sgn)
        base = b - c
        both = jnp.concatenate([src[base], src[base + 1]], axis=0)
        for half in range(2):
            scores = lax.dot_general(
                qry[pl.ds(4 * half, 4)].reshape(4 * rows, width), both,
                (((1,), (1,)), ((), ())), preferred_element_type=F32,
            )
            for i in range(4):
                for k in range(2):
                    slot = ((w - base - k + n_wide) % n_wide) * 8 + 4 * half + i
                    tile = wts[inv[slot]].astype(F32)
                    piece = scores[i * rows:(i + 1) * rows, k * rows:(k + 1) * rows]
                    pbuf[half, i * rows:(i + 1) * rows, k * rows:(k + 1) * rows] = (
                        jnp.tanh(piece * factor) * tile
                    ).astype(BF16)
            total[pl.ds(4 * half, 4)] += jnp.dot(
                pbuf[half], both, preferred_element_type=F32
            ).reshape(4, rows, width)

    def loop(lo, hi, body):
        def step(i, carry):
            body(i)
            return carry

        lax.fori_loop(lo, hi, step, 0)

    hold_first(w, 0)
    for k in range(3):
        move(w, send_z.at[k], z_peers[k]).start()
    qmove(r, 0, z_far).start()
    qmove(r, 1, x_ahead).start()
    qmove(r, 2, x_behind).start()
    forward(0, 0)
    loop(1, 4, lambda j: event(0, j))
    qgot(rep_of(zh, x - sgn))
    qmove(rep_of(zh, x - sgn), 3, x_ahead).start()
    loop(0, 2, lambda j: event(1, j))
    qgot(rep_of(zo, x))
    qmove(rep_of(zo, x), 4, x_ahead).start()
    qmove(rep_of(zo, x), 5, x_behind).start()
    loop(2, 4, lambda j: event(1, j))
    qgot(rep_of(zo, x - sgn))
    qmove(rep_of(zo, x - sgn), 6, x_ahead).start()
    event(2, 0)
    for zz in (zh, zo):
        qgot(rep_of(zz, x + sgn))
        qgot(rep_of(zz, x + 2))
    load.wait()

    loop(0, 4, pair)

    def third(j):
        event(2, j)
        loop(0, 4, lambda i: pair(4 * j + i))

    def fourth(j):
        event(3, j)
        loop(0, 2, lambda i: pair(16 + 2 * j + i))
        loop(0, 2, lambda i: pair(24 + 2 * j + i))

    loop(1, 4, third)
    loop(0, 4, fourth)

    def xcopy(a, b, k, device):
        return remote(a, b, xsend.at[k], xrecv.at[k], device)

    zs = (zo, zh)
    part[...] = total[...].astype(BF16)
    c_far = [xcopy(part.at[rep_of(zs[k], x + 2)], far.at[k], k, x_ahead) for k in (0, 1)]
    c_near = [xcopy(part.at[rep_of(zs[k], x - sgn)], near.at[k], 2 + k, x_behind) for k in (0, 1)]
    c_join = [xcopy(merged.at[k], joined.at[k], 4 + k, x_ahead) for k in (0, 1)]
    c_z = xcopy(zbuf.at[0], zbuf.at[1], 6, z_far)
    for k in (0, 1):
        c_far[k].start()
        c_near[k].start()
    for k in (0, 1):
        c_far[k].wait_recv()
        merged[k] = (total[rep_of(zs[k], x + sgn)] + far[k].astype(F32)).astype(BF16)
        c_join[k].start()

    def mine(k):
        c_near[k].wait_recv()
        c_join[k].wait_recv()
        return total[rep_of(zs[k], x)] + near[k].astype(F32) + joined[k].astype(F32)

    zbuf[0] = mine(0).astype(BF16)
    c_z.start()
    own = mine(1)
    c_z.wait_recv()
    message = (own + zbuf[1].astype(F32)).astype(BF16)
    out[...] = (
        feat[...].astype(F32) + jnp.dot(message, w_out[...], preferred_element_type=F32)
    ).astype(BF16)

    for copy in c_far + c_near + c_join + [c_z]:
        copy.wait_send()
    loop(0, 16, lambda k: move(w, send_p.at[k], ahead).wait_send())
    loop(0, 12, lambda k: move(w, send_s.at[k], behind).wait_send())
    loop(0, 3, lambda k: move(w, send_z.at[k], ahead).wait_send())
    loop(0, 32, lambda k: move(w, send_c.at[k], partner).wait_send())
    loop(0, 7, lambda k: qmove(r, k, x_ahead).wait_send())


def on_device(features, w_query, w_key, w_out, edge_weight, tile_slot, tile_count):
    rows, width = features.shape
    n_wide = lax.axis_size("wide")
    n_rep = lax.axis_size("rep")
    weights = edge_weight[0, 0]
    n_live = weights.shape[0]
    order = jnp.arange(n_live, dtype=jnp.int32)
    hit = (tile_slot[0, 0][None, :] == jnp.arange(n_wide * n_rep, dtype=jnp.int32)[:, None]) & (
        order < tile_count[0, 0]
    )[None, :]
    inv = jnp.min(jnp.where(hit, order[None, :], n_live), axis=1)
    vmem = pl.BlockSpec(memory_space=pltpu.VMEM)
    dma = pltpu.SemaphoreType.DMA
    return pl.pallas_call(
        layer_kernel,
        out_shape=jax.ShapeDtypeStruct((rows, width), BF16),
        in_specs=[vmem] * 4
        + [pl.BlockSpec(memory_space=pl.ANY), pl.BlockSpec(memory_space=pltpu.SMEM)],
        out_specs=vmem,
        scratch_shapes=[
            pltpu.VMEM((n_wide, rows, width), BF16),
            pltpu.VMEM((n_rep, rows, width), BF16),
            pltpu.VMEM((n_live + 1, rows, rows), BF16),
            pltpu.VMEM((n_rep, rows, width), F32),
            pltpu.VMEM((2, 4 * rows, 2 * rows), BF16),
            pltpu.VMEM((n_rep, rows, width), BF16),
            pltpu.VMEM((2, rows, width), BF16),
            pltpu.VMEM((2, rows, width), BF16),
            pltpu.VMEM((2, rows, width), BF16),
            pltpu.VMEM((2, rows, width), BF16),
            pltpu.VMEM((2, rows, width), BF16),
            dma((n_wide,)), dma((16,)), dma((12,)), dma((3,)), dma((32,)),
            dma((n_rep,)), dma((7,)), dma((7,)), dma((7,)), dma,
        ],
        compiler_params=pltpu.CompilerParams(
            collective_id=0, has_side_effects=True, vmem_limit_bytes=56 * 2**20
        ),
    )(features, w_query, w_key, w_out, weights, inv)


def solution(mesh):
    in_specs = (
        P(("wide", "rep"), None),
        P(),
        P(),
        P(),
        P("wide", "rep", None, None, None),
        P("wide", "rep", None),
        P("wide", "rep"),
    )
    out_specs = P(("wide", "rep"), None)
    return jax.shard_map(
        on_device, mesh=mesh, in_specs=in_specs, out_specs=out_specs, check_vma=False
    )
```

time: 350 us -> 127 us (0.36)
  the two profiles are of different devices: /device:TPU:1 before, /device:TPU:65 now
where the time goes in v2:
time: 127 us
  Pallas kernels  123 us (97%)
  local copies, waits for them, and re-layouts  1.57 us (1%)
  other arithmetic  1.37 us (1%)
    pallas_call x1, Pallas kernels, on_device(): pl.pallas_call(layer_kernel, out_shape=jax.ShapeDtypeStruct((rows, width)...  123 us

profile of v2, /device:TPU:65, one launch (start us, length us, event | category | flops | bytes accessed | tf_op | source)
XLA Modules:
  0.0 127.1 jit_solution(2446828469537140677)
XLA Ops:
  0.7 1.4 %select_reduce_fusion.inv = s32[512]{0:T(512)} fusion(s32[96]{0:T(128)} %bitcast.5, pred[96]{0:T(512)(128)(4,1)S(1)} %iota_compare_fusion.1), kind=kLoop, calls=%fused_computation | loop fusion | flops 196096 | bytes 2528 | tf_op jit(solution)/shard_map/reduce_min | solution.py:220
  2.0 123.5 %shard_map.73 = bf16[128,512]{1,0:T(8,128)(2,1)} custom-call(bf16[128,512]{1,0:T(8,128)(2,1)} %feat.1, bf16[512,512]{1,0:T(8,128)(2,1)} %w_query.1, bf16[512,512]{1,0:T(8,128)(2,1)} %w_key.1, bf16[512,512]{1,0:T(8,128)(2,1)} %w_out.1, bf16[96,128,128]{2,1,0:T(8,128)(2,1)} %bitcast.4, s32[512]{0:T(512)} %select_reduce_fusion.inv), custom_call_target="tpu_custom_call" | custom-call | tf_op jit(solution)/shard_map/pallas_call | solution.py:223
  125.5 1.6 %copy.10 = bf16[128,512]{1,0:T(8,128)(2,1)} copy(bf16[128,512]{1,0:T(8,128)(2,1)} %shard_map.73) | data formatting | bytes 262144
  (1 shorter events, 0.0 us)

commit v3 on v2

v3 whole, which is shorter than its diff:
```python
import jax
import jax.numpy as jnp
from jax import lax
from jax.experimental import pallas as pl
from jax.experimental.pallas import tpu as pltpu
from jax.sharding import PartitionSpec as P

F32 = jnp.float32
BF16 = jnp.bfloat16
MESH = pl.DeviceIdType.MESH

NY, NZ, NX = 8, 4, 4
ROWS_A = 96


def layer_kernel(
    feat, w_query, w_key, w_out, edge, inv, out,
    src, qry, wts, total, pbuf, part, far, near, merged, joined, zbuf,
    recv_a, recv_b, recv_c, ring_pa, ring_sa, ring_pb, ring_sb, line_a, line_b, send_c,
    qrecv, qsend, xrecv, xsend, local,
):
    n_wide = src.shape[0]
    rows, width = feat.shape
    n_live = edge.shape[0]
    factor = 1.0 / float(width) ** 0.5
    w, r = lax.axis_index("wide"), lax.axis_index("rep")
    c, zl, y = w % 2, (w // 2) % NZ, w // 8
    zh, x = r // NX, r % NX
    zo = 1 - zh
    sgn = 1 - 2 * c
    top = zl // 2
    inner = zl * (1 - top) + (NZ - 1 - zl) * top

    def block_of(yy, zz):
        return ((yy + 2 * NY) % NY) * 8 + zz * 2 + c

    def rep_of(zz, xx):
        return zz * NX + (xx + NX) % NX

    def line_at(p):
        return top * (NZ - 1) + (1 - 2 * top) * (p + inner * (1 - p // 2) * (1 - 2 * p))

    ahead = (block_of(y + sgn, zl), r)
    behind = (block_of(y - sgn, zl), r)
    partner = (w + sgn, r)
    above, below = (w + 2, r), (w - 2, r)
    x_ahead = (w, rep_of(zh, x + sgn))
    x_behind = (w, rep_of(zh, x - sgn))
    x_far = (w, rep_of(zh, x + 2))
    z_far = (w, rep_of(zo, x))
    has_above, has_below = zl < NZ - 1, zl > 0

    def remote(a, b, s_sem, r_sem, device):
        return pltpu.make_async_remote_copy(
            src_ref=a, dst_ref=b, send_sem=s_sem, recv_sem=r_sem,
            device_id=device, device_id_type=MESH,
        )

    def move_a(b, s_sem, device):
        ref = src.at[b, pl.ds(0, ROWS_A)]
        return remote(ref, ref, s_sem, recv_a.at[b // 2], device)

    def move_b(b, s_sem, device):
        ref = src.at[b, pl.ds(ROWS_A, rows - ROWS_A)]
        return remote(ref, ref, s_sem, recv_b.at[b // 2], device)

    def move_c(b, s_sem):
        return remote(src.at[b], src.at[b], s_sem, recv_c.at[b // 2], partner)

    def qmove(b, k, device):
        return remote(qry.at[b], qry.at[b], qsend.at[k], qrecv.at[b], device)

    barrier = pltpu.get_barrier_semaphore()

    def greet(device):
        pl.semaphore_signal(barrier, inc=1, device_id=device, device_id_type=MESH)

    talk = [ahead, behind, partner, x_ahead, x_behind, x_far, z_far]
    for device in talk:
        greet(device)

    @pl.when(has_above)
    def _():
        greet(above)

    @pl.when(has_below)
    def _():
        greet(below)

    load = pltpu.make_async_copy(edge, wts.at[pl.ds(0, n_live)], local)
    load.start()
    wts[n_live] = jnp.zeros(wts.shape[1:], BF16)
    src[w] = jnp.dot(feat[...], w_key[...], preferred_element_type=F32).astype(BF16)
    qry[r] = jnp.dot(feat[...], w_query[...], preferred_element_type=F32).astype(BF16)
    total[...] = jnp.zeros_like(total)
    pl.semaphore_wait(barrier, len(talk) + 1 + inner)

    def line_pass(move, b, zz, sems, k):
        @pl.when((zz <= zl) & has_above)
        def _():
            move(b, sems.at[2 * k], above).start()

        @pl.when((zz >= zl) & has_below)
        def _():
            move(b, sems.at[2 * k + 1], below).start()

    def got_a(b):
        move_a(b, ring_pa.at[0], ahead).wait_recv()

    def got_b(b):
        move_b(b, ring_pb.at[0], ahead).wait_recv()

    def qgot(b):
        qmove(b, 0, x_ahead).wait_recv()

    def take_near(m):
        zz = line_at(m)
        b = block_of(y, zz)
        if m:
            got_a(b)
        move_a(b, ring_pa.at[m], ahead).start()
        move_a(b, ring_sa.at[m], behind).start()
        line_pass(move_a, b, zz, line_a, m)
        if m:
            got_b(b)
        else:
            qmove(r, 0, z_far).start()
            move_b(b, ring_pb.at[0], ahead).start()
            move_b(b, ring_sb.at[0], behind).start()
        line_pass(move_b, b, zz, line_b, m)
        move_c(b, send_c.at[m]).start()

    def take_second(m):
        d, p = m // NZ, m % NZ
        zz = line_at(p)
        b = block_of(y + sgn * d, zz)
        got_a(b)

        @pl.when(d < 3)
        def _():
            move_a(b, ring_sa.at[m], behind).start()

        got_b(b)

        @pl.when((p == 0) & (d < 3))
        def _():
            move_b(b, ring_sb.at[d], behind).start()

        line_pass(move_b, b, zz, line_b, m)
        move_c(b, send_c.at[m]).start()

    def take_first(n):
        d, p = 1 + n // NZ, n % NZ
        zz = line_at(p)
        b = block_of(y - sgn * d, zz)
        got_a(b)

        @pl.when(d < 4)
        def _():
            move_a(b, ring_pa.at[NZ + n], ahead).start()

        got_b(b)

        @pl.when((p == 0) & (d < 4))
        def _():
            move_b(b, ring_pb.at[d], ahead).start()

        line_pass(move_b, b, zz, line_b, 16 + n)
        move_c(b, send_c.at[16 + n]).start()

    def event(n):
        take_second(NZ + n)
        take_first(n)

    def near_block(p):
        return block_of(y, line_at(p))

    def second_block(n):
        return block_of(y + sgn * (1 + n // NZ), line_at(n % NZ))

    def first_block(n):
        return block_of(y - sgn * (1 + n // NZ), line_at(n % NZ))

    def tiles(b1, b2, first, count, wait=True):
        if wait:
            for b in (b1, b2):
                move_c(b + sgn, send_c.at[0]).wait_recv()
        blocks = [b1 - c, b1 - c + 1, b2 - c, b2 - c + 1]
        sources = jnp.concatenate([src[b] for b in blocks], axis=0)
        scores = lax.dot_general(
            qry[pl.ds(first, count)].reshape(count * rows, width), sources,
            (((1,), (1,)), ((), ())), preferred_element_type=F32,
        )
        for i in range(count):
            for k in range(4):
                slot = ((w - blocks[k] + n_wide) % n_wide) * 8 + first + i
                tile = wts[inv[slot]].astype(F32)
                piece = scores[i * rows:(i + 1) * rows, k * rows:(k + 1) * rows]
                pbuf[i * rows:(i + 1) * rows, k * rows:(k + 1) * rows] = (
                    jnp.tanh(piece * factor) * tile
                ).astype(BF16)
        total[pl.ds(first, count)] += jnp.dot(
            pbuf[:count * rows], sources, preferred_element_type=F32
        ).reshape(count, rows, width)

    def ring_tiles(n):
        tiles(second_block(n), first_block(n), 0, 8)

    def loop(lo, hi, body):
        def step(i, carry):
            body(i)
            return carry

        lax.fori_loop(lo, hi, step, 0)

    take_near(0)
    qmove(r, 1, x_ahead).start()
    qmove(r, 2, x_behind).start()
    qmove(r, 3, x_far).start()
    take_near(1)
    event(0)
    take_near(2)
    event(1)
    take_near(3)
    event(2)
    qz = rep_of(zo, x)
    qgot(qz)
    qmove(qz, 4, x_ahead).start()
    qmove(qz, 5, x_behind).start()
    qmove(qz, 6, x_far).start()
    loop(3, 6, event)
    for zz in (zh, zo):
        for k in (sgn, -sgn, 2):
            qgot(rep_of(zz, x + k))
    load.wait()
    loop(0, 2, lambda k: tiles(near_block(2 * k), near_block(2 * k + 1), 0, 8))

    def both(n):
        event(n)
        loop(2 * n - 12, 2 * n - 10, ring_tiles)

    loop(6, 12, both)
    take_first(12)
    take_first(13)
    tiles(first_block(12), first_block(13), 0, 8)
    take_first(14)
    take_first(15)

    def xcopy(a, b, k, device):
        return remote(a, b, xsend.at[k], xrecv.at[k], device)

    zs = (zo, zh)
    c_far = [xcopy(part.at[rep_of(zs[k], x + 2)], far.at[k], k, x_ahead) for k in (0, 1)]
    c_near = [xcopy(part.at[rep_of(zs[k], x - sgn)], near.at[k], 2 + k, x_behind) for k in (0, 1)]
    c_join = [xcopy(merged.at[k], joined.at[k], 4 + k, x_ahead) for k in (0, 1)]
    c_z = xcopy(zbuf.at[0], zbuf.at[1], 6, z_far)

    for k in (0, 1):
        tiles(first_block(14), first_block(15), 4 * zs[k], 4, k == 0)
        for place in (rep_of(zs[k], x + 2), rep_of(zs[k], x - sgn)):
            part[place] = total[place].astype(BF16)
        c_far[k].start()
        c_near[k].start()
    for k in (0, 1):
        c_far[k].wait_recv()
        merged[k] = (total[rep_of(zs[k], x + sgn)] + far[k].astype(F32)).astype(BF16)
        c_join[k].start()

    def mine(k):
        c_near[k].wait_recv()
        c_join[k].wait_recv()
        return total[rep_of(zs[k], x)] + near[k].astype(F32) + joined[k].astype(F32)

    zbuf[0] = mine(0).astype(BF16)
    c_z.start()
    own = mine(1)
    c_z.wait_recv()
    message = (own + zbuf[1].astype(F32)).astype(BF16)
    out[...] = (
        feat[...].astype(F32) + jnp.dot(message, w_out[...], preferred_element_type=F32)
    ).astype(BF16)

    for copy in c_far + c_near + c_join + [c_z]:
        copy.wait_send()
    loop(0, 16, lambda k: move_a(w, ring_pa.at[k], ahead).wait_send())
    loop(0, 12, lambda k: move_a(w, ring_sa.at[k], behind).wait_send())
    loop(0, 4, lambda k: move_b(w, ring_pb.at[k], ahead).wait_send())
    loop(0, 3, lambda k: move_b(w, ring_sb.at[k], behind).wait_send())
    loop(0, 32, lambda k: move_c(w, send_c.at[k]).wait_send())
    loop(0, 7, lambda k: qmove(r, k, x_ahead).wait_send())

    def line_sent(move, sems, k):
        zz = line_at(k % NZ)

        @pl.when((zz <= zl) & has_above)
        def _():
            move(w, sems.at[2 * k], above).wait_send()

        @pl.when((zz >= zl) & has_below)
        def _():
            move(w, sems.at[2 * k + 1], below).wait_send()

    loop(0, 4, lambda k: line_sent(move_a, line_a, k))
    loop(0, 32, lambda k: line_sent(move_b, line_b, k))


def on_device(features, w_query, w_key, w_out, edge_weight, tile_slot, tile_count):
    rows, width = features.shape
    n_wide = lax.axis_size("wide")
    n_rep = lax.axis_size("rep")
    weights = edge_weight[0, 0]
    n_live = weights.shape[0]
    order = jnp.arange(n_live, dtype=jnp.int32)
    hit = (tile_slot[0, 0][None, :] == jnp.arange(n_wide * n_rep, dtype=jnp.int32)[:, None]) & (
        order < tile_count[0, 0]
    )[None, :]
    inv = jnp.min(jnp.where(hit, order[None, :], n_live), axis=1)
    vmem = pl.BlockSpec(memory_space=pltpu.VMEM)
    dma = pltpu.SemaphoreType.DMA
    return pl.pallas_call(
        layer_kernel,
        out_shape=jax.ShapeDtypeStruct((rows, width), BF16),
        in_specs=[vmem] * 4
        + [pl.BlockSpec(memory_space=pl.ANY), pl.BlockSpec(memory_space=pltpu.SMEM)],
        out_specs=vmem,
        scratch_shapes=[
            pltpu.VMEM((n_wide, rows, width), BF16),
            pltpu.VMEM((n_rep, rows, width), BF16),
            pltpu.VMEM((n_live + 1, rows, rows), BF16),
            pltpu.VMEM((n_rep, rows, width), F32),
            pltpu.VMEM((8 * rows, 4 * rows), BF16),
            pltpu.VMEM((n_rep, rows, width), BF16),
            pltpu.VMEM((2, rows, width), BF16),
            pltpu.VMEM((2, rows, width), BF16),
            pltpu.VMEM((2, rows, width), BF16),
            pltpu.VMEM((2, rows, width), BF16),
            pltpu.VMEM((2, rows, width), BF16),
            dma((32,)), dma((32,)), dma((32,)), dma((16,)), dma((12,)), dma((4,)), dma((3,)),
            dma((8,)), dma((64,)), dma((32,)),
            dma((n_rep,)), dma((7,)), dma((7,)), dma((7,)), dma,
        ],
        compiler_params=pltpu.CompilerParams(
            collective_id=0, has_side_effects=True, vmem_limit_bytes=56 * 2**20
        ),
    )(features, w_query, w_key, w_out, weights, inv)


def solution(mesh):
    in_specs = (
        P(("wide", "rep"), None),
        P(),
        P(),
        P(),
        P("wide", "rep", None, None, None),
        P("wide", "rep", None),
        P("wide", "rep"),
    )
    out_specs = P(("wide", "rep"), None)
    return jax.shard_map(
        on_device, mesh=mesh, in_specs=in_specs, out_specs=out_specs, check_vma=False
    )
```

time: 127 us -> 105 us (0.83)
  the two profiles are of different devices: /device:TPU:65 before, /device:TPU:1 now
where the time goes in v3:
time: 105 us
  Pallas kernels  101 us (96%)
  local copies, waits for them, and re-layouts  1.57 us (1%)
  other arithmetic  1.37 us (1%)
    pallas_call x1, Pallas kernels, on_device(): pl.pallas_call(layer_kernel, out_shape=jax.ShapeDtypeStruct((rows, width)...  101 us

profile of v3, /device:TPU:1, one launch (start us, length us, event | category | flops | bytes accessed | tf_op | source)
XLA Modules:
  0.0 104.8 jit_solution(11515821793559640198)
XLA Ops:
  0.7 1.4 %select_reduce_fusion.inv = s32[512]{0:T(512)} fusion(s32[96]{0:T(128)} %bitcast.5, pred[96]{0:T(512)(128)(4,1)S(1)} %iota_compare_fusion.1), kind=kLoop, calls=%fused_computation | loop fusion | flops 196096 | bytes 2528 | tf_op jit(solution)/shard_map/reduce_min | solution.py:317
  2.0 101.2 %shard_map.73 = bf16[128,512]{1,0:T(8,128)(2,1)} custom-call(bf16[128,512]{1,0:T(8,128)(2,1)} %feat.1, bf16[512,512]{1,0:T(8,128)(2,1)} %w_query.1, bf16[512,512]{1,0:T(8,128)(2,1)} %w_key.1, bf16[512,512]{1,0:T(8,128)(2,1)} %w_out.1, bf16[96,128,128]{2,1,0:T(8,128)(2,1)} %bitcast.4, s32[512]{0:T(512)} %select_reduce_fusion.inv), custom_call_target="tpu_custom_call" | custom-call | tf_op jit(solution)/shard_map/pallas_call | solution.py:320
  103.2 1.6 %copy.10 = bf16[128,512]{1,0:T(8,128)(2,1)} copy(bf16[128,512]{1,0:T(8,128)(2,1)} %shard_map.73) | data formatting | bytes 262144
  (1 shorter events, 0.0 us)

commit v4 on v3

--- a/solution.py
+++ b/solution.py
@@ -16,7 +16,8 @@
 def layer_kernel(
     feat, w_query, w_key, w_out, edge, inv, out,
     src, qry, wts, total, pbuf, part, far, near, merged, joined, zbuf,
-    recv_a, recv_b, recv_c, ring_pa, ring_sa, ring_pb, ring_sb, line_a, line_b, send_c,
+    recv_a, recv_b, recv_ca, recv_cb, ring_pa, ring_sa, ring_pb, ring_sb, line_a, line_b,
+    send_ca, send_cb,
     qrecv, qsend, xrecv, xsend, local,
 ):
     n_wide = src.shape[0]
@@ -64,8 +65,13 @@
         ref = src.at[b, pl.ds(ROWS_A, rows - ROWS_A)]
         return remote(ref, ref, s_sem, recv_b.at[b // 2], device)
 
-    def move_c(b, s_sem):
-        return remote(src.at[b], src.at[b], s_sem, recv_c.at[b // 2], partner)
+    def move_ca(b, k):
+        ref = src.at[b, pl.ds(0, ROWS_A)]
+        return remote(ref, ref, send_ca.at[k], recv_ca.at[b // 2], partner)
+
+    def move_cb(b, k):
+        ref = src.at[b, pl.ds(ROWS_A, rows - ROWS_A)]
+        return remote(ref, ref, send_cb.at[k], recv_cb.at[b // 2], partner)
 
     def qmove(b, k, device):
         return remote(qry.at[b], qry.at[b], qsend.at[k], qrecv.at[b], device)
@@ -112,6 +118,13 @@
 
     def qgot(b):
         qmove(b, 0, x_ahead).wait_recv()
+
+    def when(cond, body):
+        if isinstance(cond, bool):
+            if cond:
+                body()
+        else:
+            pl.when(cond)(body)
 
     def take_near(m):
         zz = line_at(m)
@@ -121,52 +134,58 @@
         move_a(b, ring_pa.at[m], ahead).start()
         move_a(b, ring_sa.at[m], behind).start()
         line_pass(move_a, b, zz, line_a, m)
-        if m:
-            got_b(b)
-        else:
-            qmove(r, 0, z_far).start()
-            move_b(b, ring_pb.at[0], ahead).start()
-            move_b(b, ring_sb.at[0], behind).start()
-        line_pass(move_b, b, zz, line_b, m)
-        move_c(b, send_c.at[m]).start()
+        move_ca(b, m).start()
 
     def take_second(m):
         d, p = m // NZ, m % NZ
-        zz = line_at(p)
-        b = block_of(y + sgn * d, zz)
+        b = block_of(y + sgn * d, line_at(p))
         got_a(b)
-
-        @pl.when(d < 3)
-        def _():
-            move_a(b, ring_sa.at[m], behind).start()
-
-        got_b(b)
-
-        @pl.when((p == 0) & (d < 3))
-        def _():
-            move_b(b, ring_sb.at[d], behind).start()
-
-        line_pass(move_b, b, zz, line_b, m)
-        move_c(b, send_c.at[m]).start()
+        when(d < 3, lambda: move_a(b, ring_sa.at[m], behind).start())
+        move_ca(b, m).start()
 
     def take_first(n):
         d, p = 1 + n // NZ, n % NZ
+        b = block_of(y - sgn * d, line_at(p))
+        got_a(b)
+        when(d < 4, lambda: move_a(b, ring_pa.at[NZ + n], ahead).start())
+        move_ca(b, 16 + n).start()
+
+    def rest(d, p):
         zz = line_at(p)
-        b = block_of(y - sgn * d, zz)
-        got_a(b)
-
-        @pl.when(d < 4)
-        def _():
-            move_a(b, ring_pa.at[NZ + n], ahead).start()
-
-        got_b(b)
-
-        @pl.when((p == 0) & (d < 4))
-        def _():
-            move_b(b, ring_pb.at[d], ahead).start()
-
-        line_pass(move_b, b, zz, line_b, 16 + n)
-        move_c(b, send_c.at[16 + n]).start()
+
+        def near():
+            b = block_of(y, zz)
+            if p:
+                got_b(b)
+            else:
+                move_b(b, ring_pb.at[0], ahead).start()
+                move_b(b, ring_sb.at[0], behind).start()
+            line_pass(move_b, b, zz, line_b, p)
+            move_cb(b, p).start()
+
+        def second():
+            b = block_of(y + sgn * d, zz)
+            got_b(b)
+            if p == 0:
+                when(d < 3, lambda: move_b(b, ring_sb.at[d], behind).start())
+            line_pass(move_b, b, zz, line_b, 4 * d + p)
+            move_cb(b, 4 * d + p).start()
+
+        def first():
+            b = block_of(y - sgn * d, zz)
+            got_b(b)
+            if p == 0:
+                when(d < 4, lambda: move_b(b, ring_pb.at[d], ahead).start())
+            line_pass(move_b, b, zz, line_b, 12 + 4 * d + p)
+            move_cb(b, 12 + 4 * d + p).start()
+
+        when(d == 0, near)
+        when((d >= 1) & (d <= 3), second)
+        when((d >= 1) & (d <= 4), first)
+
+    def diagonal(k):
+        for p in range(NZ):
+            rest(k - p, p)
 
     def event(n):
         take_second(NZ + n)
@@ -184,7 +203,8 @@
     def tiles(b1, b2, first, count, wait=True):
         if wait:
             for b in (b1, b2):
-                move_c(b + sgn, send_c.at[0]).wait_recv()
+                move_ca(b + sgn, 0).wait_recv()
+                move_cb(b + sgn, 0).wait_recv()
         blocks = [b1 - c, b1 - c + 1, b2 - c, b2 - c + 1]
         sources = jnp.concatenate([src[b] for b in blocks], axis=0)
         scores = lax.dot_general(
@@ -214,32 +234,43 @@
         lax.fori_loop(lo, hi, step, 0)
 
     take_near(0)
+    qmove(r, 0, z_far).start()
     qmove(r, 1, x_ahead).start()
     qmove(r, 2, x_behind).start()
     qmove(r, 3, x_far).start()
+    rest(0, 0)
     take_near(1)
     event(0)
+    diagonal(1)
     take_near(2)
     event(1)
     take_near(3)
     event(2)
+    diagonal(2)
     qz = rep_of(zo, x)
     qgot(qz)
     qmove(qz, 4, x_ahead).start()
     qmove(qz, 5, x_behind).start()
     qmove(qz, 6, x_far).start()
-    loop(3, 6, event)
+    event(3)
+    event(4)
+    diagonal(3)
+    event(5)
     for zz in (zh, zo):
         for k in (sgn, -sgn, 2):
             qgot(rep_of(zz, x + k))
     load.wait()
     loop(0, 2, lambda k: tiles(near_block(2 * k), near_block(2 * k + 1), 0, 8))
 
-    def both(n):
-        event(n)
-        loop(2 * n - 12, 2 * n - 10, ring_tiles)
-
-    loop(6, 12, both)
+    def both(t):
+        event(6 + 2 * t)
+        diagonal(4 + t)
+        loop(4 * t, 4 * t + 2, ring_tiles)
+        event(7 + 2 * t)
+        loop(4 * t + 2, 4 * t + 4, ring_tiles)
+
+    loop(0, 3, both)
+    diagonal(7)
     take_first(12)
     take_first(13)
     tiles(first_block(12), first_block(13), 0, 8)
@@ -286,7 +317,8 @@
     loop(0, 12, lambda k: move_a(w, ring_sa.at[k], behind).wait_send())
     loop(0, 4, lambda k: move_b(w, ring_pb.at[k], ahead).wait_send())
     loop(0, 3, lambda k: move_b(w, ring_sb.at[k], behind).wait_send())
-    loop(0, 32, lambda k: move_c(w, send_c.at[k]).wait_send())
+    loop(0, 32, lambda k: move_ca(w, k).wait_send())
+    loop(0, 32, lambda k: move_cb(w, k).wait_send())
     loop(0, 7, lambda k: qmove(r, k, x_ahead).wait_send())
 
     def line_sent(move, sems, k):
@@ -335,8 +367,8 @@
             pltpu.VMEM((2, rows, width), BF16),
             pltpu.VMEM((2, rows, width), BF16),
             pltpu.VMEM((2, rows, width), BF16),
-            dma((32,)), dma((32,)), dma((32,)), dma((16,)), dma((12,)), dma((4,)), dma((3,)),
-            dma((8,)), dma((64,)), dma((32,)),
+            dma((32,)), dma((32,)), dma((32,)), dma((32,)), dma((16,)), dma((12,)), dma((4,)),
+            dma((3,)), dma((8,)), dma((64,)), dma((32,)), dma((32,)),
             dma((n_rep,)), dma((7,)), dma((7,)), dma((7,)), dma,
         ],
         compiler_params=pltpu.CompilerParams(

time: 105 us -> 94.8 us (0.903)
  Pallas kernels: 101 us -> 91 us
    pallas_call x1, Pallas kernels: 101 us -> 91 us  [on_device(): pl.pallas_call(layer_kernel, out_shape=jax.ShapeDtypeStruct((rows, width)...]
where the time goes in v4:
time: 94.8 us; the launch traced here: 94.6 us
  Pallas kernels  91 us (96%)
  local copies, waits for them, and re-layouts  1.57 us (2%)
  other arithmetic  1.37 us (1%)
    pallas_call x1, Pallas kernels, on_device(): pl.pallas_call(layer_kernel, out_shape=jax.ShapeDtypeStruct((rows, width)...  91 us

profile of v4, /device:TPU:1, one launch (start us, length us, event | category | flops | bytes accessed | tf_op | source)
XLA Modules:
  0.0 94.6 jit_solution(5906136736889116384)
XLA Ops:
  0.7 1.4 %select_reduce_fusion.inv = s32[512]{0:T(512)} fusion(s32[96]{0:T(128)} %bitcast.5, pred[96]{0:T(512)(128)(4,1)S(1)} %iota_compare_fusion.1), kind=kLoop, calls=%fused_computation | loop fusion | flops 196096 | bytes 2528 | tf_op jit(solution)/shard_map/reduce_min | solution.py:349
  2.0 91.0 %shard_map.73 = bf16[128,512]{1,0:T(8,128)(2,1)} custom-call(bf16[128,512]{1,0:T(8,128)(2,1)} %feat.1, bf16[512,512]{1,0:T(8,128)(2,1)} %w_query.1, bf16[512,512]{1,0:T(8,128)(2,1)} %w_key.1, bf16[512,512]{1,0:T(8,128)(2,1)} %w_out.1, bf16[96,128,128]{2,1,0:T(8,128)(2,1)} %bitcast.4, s32[512]{0:T(512)} %select_reduce_fusion.inv), custom_call_target="tpu_custom_call" | custom-call | tf_op jit(solution)/shard_map/pallas_call | solution.py:352
  93.0 1.6 %copy.10 = bf16[128,512]{1,0:T(8,128)(2,1)} copy(bf16[128,512]{1,0:T(8,128)(2,1)} %shard_map.73) | data formatting | bytes 262144
  (1 shorter events, 0.0 us)

commit v5 on v4

--- a/solution.py
+++ b/solution.py
@@ -14,11 +14,11 @@
 
 
 def layer_kernel(
-    feat, w_query, w_key, w_out, edge, inv, out,
+    feat, w_query, w_key, w_out, edge, slots, count, out,
     src, qry, wts, total, pbuf, part, far, near, merged, joined, zbuf,
     recv_a, recv_b, recv_ca, recv_cb, ring_pa, ring_sa, ring_pb, ring_sb, line_a, line_b,
     send_ca, send_cb,
-    qrecv, qsend, xrecv, xsend, local,
+    qrecv, qsend, xrecv, xsend, local, found, table, listed,
 ):
     n_wide = src.shape[0]
     rows, width = feat.shape
@@ -99,7 +99,18 @@
     src[w] = jnp.dot(feat[...], w_key[...], preferred_element_type=F32).astype(BF16)
     qry[r] = jnp.dot(feat[...], w_query[...], preferred_element_type=F32).astype(BF16)
     total[...] = jnp.zeros_like(total)
+
+    numbers = lax.broadcasted_iota(jnp.int32, found.shape, 0) * found.shape[1]
+    numbers += lax.broadcasted_iota(jnp.int32, found.shape, 1)
+    live = count[0]
+
+    def look(t, held):
+        return jnp.where(numbers == jnp.where(t < live, slots[t], -1), t, held)
+
+    found[...] = lax.fori_loop(0, n_live, look, jnp.full(found.shape, n_live, jnp.int32))
     pl.semaphore_wait(barrier, len(talk) + 1 + inner)
+
+    fetch = pltpu.make_async_copy(found, table, listed)
 
     def line_pass(move, b, zz, sems, k):
         @pl.when((zz <= zl) & has_above)
@@ -214,7 +225,7 @@
         for i in range(count):
             for k in range(4):
                 slot = ((w - blocks[k] + n_wide) % n_wide) * 8 + first + i
-                tile = wts[inv[slot]].astype(F32)
+                tile = wts[table[slot // 128, slot % 128]].astype(F32)
                 piece = scores[i * rows:(i + 1) * rows, k * rows:(k + 1) * rows]
                 pbuf[i * rows:(i + 1) * rows, k * rows:(k + 1) * rows] = (
                     jnp.tanh(piece * factor) * tile
@@ -239,6 +250,7 @@
     qmove(r, 2, x_behind).start()
     qmove(r, 3, x_far).start()
     rest(0, 0)
+    fetch.start()
     take_near(1)
     event(0)
     diagonal(1)
@@ -260,6 +272,7 @@
         for k in (sgn, -sgn, 2):
             qgot(rep_of(zz, x + k))
     load.wait()
+    fetch.wait()
     loop(0, 2, lambda k: tiles(near_block(2 * k), near_block(2 * k + 1), 0, 8))
 
     def both(t):
@@ -290,12 +303,17 @@
         tiles(first_block(14), first_block(15), 4 * zs[k], 4, k == 0)
         for place in (rep_of(zs[k], x + 2), rep_of(zs[k], x - sgn)):
             part[place] = total[place].astype(BF16)
-        c_far[k].start()
         c_near[k].start()
-    for k in (0, 1):
+        if k == 0:
+            c_far[0].start()
+
+    def join(k):
         c_far[k].wait_recv()
         merged[k] = (total[rep_of(zs[k], x + sgn)] + far[k].astype(F32)).astype(BF16)
         c_join[k].start()
+
+    join(0)
+    c_far[1].start()
 
     def mine(k):
         c_near[k].wait_recv()
@@ -304,6 +322,7 @@
 
     zbuf[0] = mine(0).astype(BF16)
     c_z.start()
+    join(1)
     own = mine(1)
     c_z.wait_recv()
     message = (own + zbuf[1].astype(F32)).astype(BF16)
@@ -342,18 +361,14 @@
     n_rep = lax.axis_size("rep")
     weights = edge_weight[0, 0]
     n_live = weights.shape[0]
-    order = jnp.arange(n_live, dtype=jnp.int32)
-    hit = (tile_slot[0, 0][None, :] == jnp.arange(n_wide * n_rep, dtype=jnp.int32)[:, None]) & (
-        order < tile_count[0, 0]
-    )[None, :]
-    inv = jnp.min(jnp.where(hit, order[None, :], n_live), axis=1)
     vmem = pl.BlockSpec(memory_space=pltpu.VMEM)
     dma = pltpu.SemaphoreType.DMA
     return pl.pallas_call(
         layer_kernel,
         out_shape=jax.ShapeDtypeStruct((rows, width), BF16),
         in_specs=[vmem] * 4
-        + [pl.BlockSpec(memory_space=pl.ANY), pl.BlockSpec(memory_space=pltpu.SMEM)],
+        + [pl.BlockSpec(memory_space=pl.ANY)]
+        + [pl.BlockSpec(memory_space=pltpu.SMEM)] * 2,
         out_specs=vmem,
         scratch_shapes=[
             pltpu.VMEM((n_wide, rows, width), BF16),
@@ -370,11 +385,13 @@
             dma((32,)), dma((32,)), dma((32,)), dma((32,)), dma((16,)), dma((12,)), dma((4,)),
             dma((3,)), dma((8,)), dma((64,)), dma((32,)), dma((32,)),
             dma((n_rep,)), dma((7,)), dma((7,)), dma((7,)), dma,
+            pltpu.VMEM((n_wide * n_rep // 128, 128), jnp.int32),
+            pltpu.SMEM((n_wide * n_rep // 128, 128), jnp.int32), dma,
         ],
         compiler_params=pltpu.CompilerParams(
             collective_id=0, has_side_effects=True, vmem_limit_bytes=56 * 2**20
         ),
-    )(features, w_query, w_key, w_out, weights, inv)
+    )(features, w_query, w_key, w_out, weights, tile_slot[0, 0], tile_count[0])
 
 
 def solution(mesh):

time: 94.8 us -> 92.2 us (0.973)
  the two profiles are of different devices: /device:TPU:1 before, /device:TPU:28 now
where the time goes in v5:
time: 92.2 us; the launch traced here: 92.1 us
  Pallas kernels  89.9 us (98%)
  local copies, waits for them, and re-layouts  1.57 us (2%)
    pallas_call x1, Pallas kernels, on_device(): pl.pallas_call(layer_kernel, out_shape=jax.ShapeDtypeStruct((rows, width)...  89.9 us

profile of v5, /device:TPU:28, one launch (start us, length us, event | category | flops | bytes accessed | tf_op | source)
XLA Modules:
  0.0 92.1 jit_solution(6443984577022180781)
XLA Ops:
  0.7 89.9 %shard_map.73 = bf16[128,512]{1,0:T(8,128)(2,1)} custom-call(bf16[128,512]{1,0:T(8,128)(2,1)} %feat.1, bf16[512,512]{1,0:T(8,128)(2,1)} %w_query.1, bf16[512,512]{1,0:T(8,128)(2,1)} %w_key.1, bf16[512,512]{1,0:T(8,128)(2,1)} %w_out.1, bf16[96,128,128]{2,1,0:T(8,128)(2,1)} %bitcast.4, s32[96]{0:T(128)} %bitcast.5, s32[1]{0:T(128)} %bitcast.3.count), custom_call_target="tpu_custom_call" | custom-call | tf_op jit(solution)/shard_map/pallas_call | solution.py:366
  90.5 1.6 %copy.10 = bf16[128,512]{1,0:T(8,128)(2,1)} copy(bf16[128,512]{1,0:T(8,128)(2,1)} %shard_map.73) | data formatting | bytes 262144
